TPU v7x, 256 devices: a whole 4x4x8 slice. The times are simulated.
256 devices in a mesh: row: 16 (over x, z_hi, core), col: 16 (over z_lo, y).
Axes of the slice: x: 4, y: 4, z: 8 (z_hi: 2, z_lo: 4; z = z_hi * 4 + z_lo), core: 2. Of those that a mesh axis runs over, the one named last changes fastest.
Arguments:
- diag_coords: int32 [2, 1536], replicated, may hold values from 0 to 32767
- panel_coords: int32 [2, 16, 1536], P(None, 'row', 'col'), may hold values from 0 to 32767
- test_matrix: bfloat16 [16, 1536, 512], P('row', 'col'), may hold values from -6 to 6
- ranks: int32 [16], replicated, may hold values from 64 to 512, as said below
Outputs:
- panel_left: bfloat16 [16, 1536, 512], P('row', 'col')
- update_right: bfloat16 [16, 16, 1536, 512], P('row', 'col')
Inputs may be any that keep to these rules, and one draw needn't show every extreme that they name: ranks[i] is 512 at tile 0 and 64 at the last tile and falls roughly evenly in between, with small random steps.
All inputs are finite; a program needn't handle non-finite values.
Results may differ from a plain program's by a relative error of at most 0.0068.
Values may be sent and summed in bfloat16 or wider, within the bound.
No kernel may reach another device: no remote copies, remote signals or barrier semaphores. Data moves between devices by JAX's collectives and lax.ppermute only.
A program may use at most 192 MiB of HBM per device.

v0:
```python
import jax
import jax.numpy as jnp
from jax import lax
from jax.sharding import PartitionSpec as P

range_length = 409.6
nugget = 0.5
shift_ratio = 0.01


def broadcast(value, axis, root):
    mine = lax.axis_index(axis) == root
    return lax.psum(jnp.where(mine, value, jnp.zeros_like(value)), axis)


def matern(first, second):
    delta_x = (first[0][:, None] - second[0][None, :]).astype(jnp.float32)
    delta_y = (first[1][:, None] - second[1][None, :]).astype(jnp.float32)
    return jnp.exp(-jnp.sqrt(delta_x * delta_x + delta_y * delta_y) / range_length)


def solve_right(factor, sample):
    return jax.scipy.linalg.solve_triangular(factor, sample.T, lower=True).T


def shards(diag_coords, panel_coords, test_matrix, ranks):
    points = diag_coords.shape[1]
    row_tiles = panel_coords.shape[1]
    width = test_matrix.shape[2]
    n_row = lax.axis_size("row")
    n_col = lax.axis_size("col")
    col_tiles = row_tiles * n_row // n_col
    row_index = lax.axis_index("row")
    col_index = lax.axis_index("col")
    cov = matern(diag_coords, diag_coords) + nugget * jnp.eye(points, dtype=jnp.float32)
    is_owner = (row_index == 0) & (col_index == 0)
    lower = lax.cond(is_owner, jnp.linalg.cholesky, jnp.zeros_like, cov)
    lower = broadcast(lower, ("row", "col"), 0)
    columns = jnp.arange(width, dtype=jnp.int32)
    row_ranks = lax.dynamic_slice_in_dim(ranks, row_index * row_tiles, row_tiles)
    row_mask = (columns[None, :] < row_ranks[:, None]).astype(jnp.float32)
    tests_full = lax.all_gather(test_matrix, "col", axis=1, tiled=True)
    tests_rows = tests_full * row_mask.astype(jnp.bfloat16)[:, None, :]
    local_points = panel_coords.reshape(2, -1)
    block = matern(local_points, diag_coords)
    solved = jax.scipy.linalg.solve_triangular(lower, block.T, lower=True).T
    solved = solved.reshape(row_tiles, -1, points)
    sample = jnp.einsum(
        "inm,imr->inr", solved, tests_rows.astype(jnp.float32), precision=lax.Precision.HIGHEST
    )
    gram_part = jnp.einsum("inr,ins->irs", sample, sample, precision=lax.Precision.HIGHEST)
    gram = lax.psum(gram_part, "col")
    trace = jnp.sum(jnp.diagonal(gram, axis1=1, axis2=2), axis=1)
    shift = shift_ratio * trace / row_ranks.astype(jnp.float32)
    extra = shift[:, None] * row_mask + 1.0 - row_mask
    shifted = gram + extra[:, :, None] * jnp.eye(width, dtype=jnp.float32)[None]
    factor = jnp.linalg.cholesky(shifted)
    left = jax.vmap(solve_right)(factor, sample).astype(jnp.bfloat16)
    coeff_part = jnp.einsum(
        "inm,inr->imr", solved, left.astype(jnp.float32), precision=lax.Precision.HIGHEST
    )
    coeff_piece = lax.psum_scatter(coeff_part, "col", scatter_dimension=1, tiled=True).astype(
        jnp.bfloat16
    )
    coeff = lax.all_gather(coeff_piece, "col", axis=1, tiled=True)
    left_full = lax.all_gather(left, "col", axis=1, tiled=True)
    root = col_index * col_tiles // row_tiles
    stacked = jnp.stack([left_full, coeff])
    slab = broadcast(stacked, "row", root)
    offset = col_index * col_tiles % row_tiles
    col_left = slab[0]
    col_coeff = slab[1]
    core = jnp.einsum("inr,jns->ijrs", coeff, col_coeff, preferred_element_type=jnp.float32)
    core = core.astype(jnp.bfloat16)
    update = jnp.einsum("jns,ijrs->ijnr", col_left, core, preferred_element_type=jnp.float32)
    return (left, update.astype(jnp.bfloat16))


def solution(mesh):
    in_specs = (P(), P(None, "row", "col"), P("row", "col", None), P())
    out_specs = (P("row", "col", None), P("row", "col", None, None))
    return jax.shard_map(shards, mesh=mesh, in_specs=in_specs, out_specs=out_specs, check_vma=False)
```

profile of v0, /device:TPU:24, one launch (start us, length us, event | category | flops | bytes accessed | tf_op | source)
XLA Modules:
  0.0 1680.3 jit_solution(12171304196142821972)
XLA Ops:
  8.9 7.0 subtract_convert_fusion
  20.2 4.8 triangular_solve.302
  25.0 4.8 broadcast.804
  29.8 14.6 conditional.1
  29.8 4.8 broadcast.796
  51.7 639.4 %all-reduce.6.cloned.1.call-done = f32[1536,1536]{1,0:T(8,128)} async-done(((f32[1536,1536]{1,0:T(8,128)}), f32[1536,1536]{1,0:T(8,128)}) %all-reduce.6.cloned.1.call-update) | async-done | bytes 9437200 | tf_op jit(solution)/shard_map/psum | solution.py:13
  691.1 8.4 fusion.72
  699.4 35.7 %while.2 = (s32[]{:T(128)}, f32[1536,1536]{1,0:T(8,128)}, s32[12,2]{0,1:T(2,128)S(1)}, f32[12,128,128]{2,1,0:T(8,128)S(1)}, s32[]{:T(128)}) while((s32[]{:T(128)}, f32[1536,1536]{1,0:T(8,128)}, s32[12,2]{0,1:T(2,128)S(1)}, f32[12,128,128]{2,1,0:T(8,128)S(1)}, s32[]{:T(128)}) %tuple.143), condition=%wide.while_cond, body=%wide.while_body.sunk | while | flops 2 | bytes 131181 | solution.py:46
  735.2 117.9 %custom-call.130 = f32[12,128,128]{1,2,0:T(8,128)S(1)} custom-call(f32[12,128,128]{2,1,0:T(8,128)S(1)} %get-tuple-element.41), custom_call_target="InvertDiagBlocksLowerTriangular" | custom-call | tf_op jit(solution)/shard_map/jit(_solve_triangular)/triangular_solve | solution.py:46
  878.2 157.0 %all-reduce.8.cloned.1.call-done = f32[1,512,512]{1,2,0:T(8,128)} async-done(((f32[1,512,512]{1,2,0:T(8,128)}), f32[1,512,512]{1,2,0:T(8,128)}) %all-reduce.8.cloned.1.call-update) | async-done | bytes 1048592 | tf_op jit(solution)/shard_map/psum | solution.py:52
  1035.3 8.6 gather_fusion
  1049.0 11.7 custom-call.131
  1060.8 9.8 custom-call.132
  1071.4 11.7 custom-call.133
  1083.5 10.0 custom-call.134
  1094.4 11.7 custom-call.135
  1106.3 9.8 custom-call.136
  1116.9 11.9 custom-call.137
  1134.3 11.3 while.3
  1145.6 40.1 %custom-call.138 = f32[1,4,128,128]{2,3,1,0:T(8,128)S(1)} custom-call(f32[1,4,128,128]{3,2,1,0:T(8,128)} %bitcast.372), custom_call_target="InvertDiagBlocksLowerTriangular" | custom-call | tf_op jit(solution)/shard_map/vmap(jit(_solve_triangular))/triangular_solve | solution.py:23
  1192.3 83.5 %reduce-scatter.2.cloned.1.call-done = f32[1,96,512]{2,1,0:T(8,128)} async-done(((f32[1,1536,512]{2,1,0:T(8,128)}), f32[1,96,512]{2,1,0:T(8,128)}) %reduce-scatter.2.cloned.1.call-update) | async-done | bytes 196624 | tf_op jit(solution)/shard_map/reduce_scatter | solution.py:62
  1277.5 84.0 %all-gather.6.cloned.1.call-done = bf16[1,1536,512]{2,1,0:T(8,128)(2,1)} async-done(((bf16[1,96,512]{2,1,0:T(8,128)(2,1)}), bf16[1,1536,512]{2,1,0:T(8,128)(2,1)}) %all-gather.6.cloned.1.call-update) | async-done | bytes 1572880 | tf_op jit(solution)/shard_map/all_gather | solution.py:66
  1361.5 83.2 %all-gather.8.cloned.1.call-done = bf16[1,1536,512]{2,1,0:T(8,128)(2,1)} async-done(((bf16[1,96,512]{2,1,0:T(8,128)(2,1)}), bf16[1,1536,512]{2,1,0:T(8,128)(2,1)}) %all-gather.8.cloned.1.call-update) | async-done | bytes 1572880 | tf_op jit(solution)/shard_map/all_gather | solution.py:65
  1448.7 218.2 %all-reduce.10.cloned.1.call-done = bf16[2,1,1536,512]{3,2,1,0:T(8,128)(2,1)} async-done(((bf16[2,1,1536,512]{3,2,1,0:T(8,128)(2,1)}), bf16[2,1,1536,512]{3,2,1,0:T(8,128)(2,1)}) %all-reduce.10.cloned.1.call-update) | async-done | bytes 3145744 | tf_op jit(solution)/shard_map/psum | solution.py:13
  (164 shorter events, 111.3 us)
Async XLA Ops:
  8.0 683.1 %all-reduce.6.cloned.1.call-start = ((), (), s32[]{:S(2)}) async-start(), calls=%async_computation.1 | async-start | bytes 18874368 | tf_op jit(solution)/shard_map/psum | solution.py:13
  49.1 0.7 copy-start.2
  49.1 0.7 copy-start.3
  49.1 823.8 %all-gather.4.cloned.1.call-start = ((), (), s32[]{:S(2)}) async-start(), calls=%async_computation.2 | async-start | bytes 1671168 | tf_op jit(solution)/shard_map/all_gather | solution.py:42
  49.7 985.5 %all-reduce.8.cloned.1.call-start = ((), (), s32[]{:S(2)}) async-start(), calls=%async_computation.3 | async-start | bytes 2097152 | tf_op jit(solution)/shard_map/psum | solution.py:52
  872.9 172.3 %copy-start = (f32[1536,96]{0,1:T(8,128)}, f32[1536,96]{0,1:T(8,128)S(1)}, u32[]{:S(2)}) copy-start(f32[1536,96]{0,1:T(8,128)S(1)} %convolution_dynamic-update-slice_fusion.10) | copy-start | bytes 1769476
  877.4 398.4 %reduce-scatter.2.cloned.1.call-start = ((), (), s32[]{:S(2)}) async-start(), calls=%async_computation.5 | async-start | bytes 3342336 | tf_op jit(solution)/shard_map/reduce_scatter | solution.py:62
  1191.5 170.0 %all-gather.6.cloned.1.call-start = ((), (), s32[]{:S(2)}) async-start(), calls=%async_computation.4 | async-start | bytes 1671168 | tf_op jit(solution)/shard_map/all_gather | solution.py:66
  1192.3 252.4 %all-gather.8.cloned.1.call-start = ((), (), s32[]{:S(2)}) async-start(), calls=%async_computation.6 | async-start | bytes 1671168 | tf_op jit(solution)/shard_map/all_gather | solution.py:65
  1277.5 389.4 %all-reduce.10.cloned.1.call-start = ((), (), s32[]{:S(2)}) async-start(), calls=%async_computation.7 | async-start | bytes 6291456 | tf_op jit(solution)/shard_map/psum | solution.py:13
  1444.7 222.2 %copy-start.1 = (bf16[1,1536,512]{2,1,0:T(8,128)(2,1)S(1)}, bf16[1,1536,512]{2,1,0:T(8,128)(2,1)}, u32[]{:S(2)}) copy-start(bf16[1,1536,512]{2,1,0:T(8,128)(2,1)} %all-gather.8.cloned.1.call-done) | copy-start | bytes 4718596
Sparse Core Ops, SparseCore 0:
  49.3 641.7 all-reduce.5
  1448.8 218.0 all-reduce.9
Sparse Core Ops, SparseCore 1:
  51.4 440.1 all-gather.3
  877.5 157.7 all-reduce.7
  1191.6 84.2 reduce-scatter.1
  1278.3 83.2 all-gather.5
  1363.9 80.7 all-gather.7
where the time goes:
time: 1690 us; the launch traced here: 1680 us
  waiting for transfers between devices  1270 us (75%)
  other arithmetic  269 us (16%)
  local copies, waits for them, and re-layouts  78.2 us (5%)
  matrix products  36 us (2%)
  between operations  20.7 us (1%)
    psum x2, waiting for transfers between devices, broadcast(): return lax.psum(jnp.where(mine, value, jnp.zeros_like(value)), axis)  858 us
    psum x1, waiting for transfers between devices, shards(): gram = lax.psum(gram_part, 'col')  157 us
    another operation x3, other arithmetic, shards(): solved = jax.scipy.linalg.solve_triangular(lower, block.T, lower=True).T  126 us
    all_gather x1, waiting for transfers between devices, shards(): left_full = lax.all_gather(left, 'col', axis=1, tiled=True)  84 us
    reduce_scatter x1, waiting for transfers between devices, shards(): lax.psum_scatter(coeff_part, 'col', scatter_dimension=1, tiled=True)  83.5 us
    all_gather x1, waiting for transfers between devices, shards(): coeff = lax.all_gather(coeff_piece, 'col', axis=1, tiled=True)  83.2 us
    another operation x15, other arithmetic, shards(): factor = jnp.linalg.cholesky(shifted)  79.4 us
    another operation x58, local copies, waits for them, and re-layouts  56.4 us
  transfers between devices with their start and end apart: 7, of which 6 were waited for; matrix products, arithmetic and copies ran while one was open for 11% of the time, Pallas kernels for 0%

commit v1 on v0

--- a/solution.py
+++ b/solution.py
@@ -63,7 +63,9 @@
         jnp.bfloat16
     )
     coeff = lax.all_gather(coeff_piece, "col", axis=1, tiled=True)
-    left_full = lax.all_gather(left, "col", axis=1, tiled=True)
+    e_next = jnp.stack([left for _ in range(jax.lax.axis_size("col"))], 0)
+    after = jax.lax.all_to_all(e_next, "col", split_axis=0, concat_axis=0)
+    left_full = jnp.concatenate(after, 1)
     root = col_index * col_tiles // row_tiles
     stacked = jnp.stack([left_full, coeff])
     slab = broadcast(stacked, "row", root)

time: 1690 us -> 1610 us (0.953)
  waiting for transfers between devices: 1270 us -> 1180 us
    all_gather x1 -> x0, waiting for transfers between devices: 84 us -> none  [shards(): left_full = lax.all_gather(left, 'col', axis=1, tiled=True)]
    another operation x58 -> x59, local copies, waits for them, and re-layouts: 56.4 us -> 57.7 us
  transfers between devices with their start and end apart: 7 -> 7, of which waited for: 6 -> 5; matrix products, arithmetic and copies ran while one was open for 11% -> 12% of each run, Pallas kernels for 0% -> 0%
where the time goes in v1:
time: 1610 us; the launch traced here: 1600 us
  waiting for transfers between devices  1180 us (73%)
  other arithmetic  269 us (17%)
  local copies, waits for them, and re-layouts  79.5 us (5%)
  matrix products  35.8 us (2%)
  between operations  20.6 us (1%)
    psum x2, waiting for transfers between devices, broadcast(): return lax.psum(jnp.where(mine, value, jnp.zeros_like(value)), axis)  858 us
    psum x1, waiting for transfers between devices, shards(): gram = lax.psum(gram_part, 'col')  157 us
    another operation x3, other arithmetic, shards(): solved = jax.scipy.linalg.solve_triangular(lower, block.T, lower=True).T  126 us
    all_gather x1, waiting for transfers between devices, shards(): coeff = lax.all_gather(coeff_piece, 'col', axis=1, tiled=True)  80.8 us
    reduce_scatter x1, waiting for transfers between devices, shards(): lax.psum_scatter(coeff_part, 'col', scatter_dimension=1, tiled=True)  79.6 us
    another operation x15, other arithmetic, shards(): factor = jnp.linalg.cholesky(shifted)  79.5 us
    another operation x58, local copies, waits for them, and re-layouts  56.4 us
    another operation x3, other arithmetic, solve_right(): return jax.scipy.linalg.solve_triangular(factor, sample.T, lower=True).T  40.3 us
  transfers between devices with their start and end apart: 7, of which 5 were waited for; matrix products, arithmetic and copies ran while one was open for 12% of the time, Pallas kernels for 0%

profile of v1, /device:TPU:24, one launch (start us, length us, event | category | flops | bytes accessed | tf_op | source)
XLA Modules:
  0.0 1601.6 jit_solution(1971227600865160873)
XLA Ops:
  8.9 7.0 subtract_convert_fusion
  20.2 4.8 triangular_solve.302
  25.0 4.8 broadcast.807
  29.8 14.1 conditional.1
  29.8 4.8 broadcast.799
  51.1 640.0 %all-reduce.6.cloned.1.call-done = f32[1536,1536]{1,0:T(8,128)} async-done(((f32[1536,1536]{1,0:T(8,128)}), f32[1536,1536]{1,0:T(8,128)}) %all-reduce.6.cloned.1.call-update) | async-done | bytes 9437200 | tf_op jit(solution)/shard_map/psum | solution.py:13
  691.1 8.4 fusion.72
  699.5 35.7 %while.2 = (s32[]{:T(128)}, f32[1536,1536]{1,0:T(8,128)}, s32[12,2]{0,1:T(2,128)S(1)}, f32[12,128,128]{2,1,0:T(8,128)S(1)}, s32[]{:T(128)}) while((s32[]{:T(128)}, f32[1536,1536]{1,0:T(8,128)}, s32[12,2]{0,1:T(2,128)S(1)}, f32[12,128,128]{2,1,0:T(8,128)S(1)}, s32[]{:T(128)}) %tuple.146), condition=%wide.while_cond, body=%wide.while_body.sunk | while | flops 2 | bytes 131181 | solution.py:46
  735.2 117.9 %custom-call.130 = f32[12,128,128]{1,2,0:T(8,128)S(1)} custom-call(f32[12,128,128]{2,1,0:T(8,128)S(1)} %get-tuple-element.41), custom_call_target="InvertDiagBlocksLowerTriangular" | custom-call | tf_op jit(solution)/shard_map/jit(_solve_triangular)/triangular_solve | solution.py:46
  877.9 157.0 %all-reduce.8.cloned.1.call-done = f32[1,512,512]{1,2,0:T(8,128)} async-done(((f32[1,512,512]{1,2,0:T(8,128)}), f32[1,512,512]{1,2,0:T(8,128)}) %all-reduce.8.cloned.1.call-update) | async-done | bytes 1048592 | tf_op jit(solution)/shard_map/psum | solution.py:52
  1034.9 8.6 gather_fusion
  1048.7 11.7 custom-call.131
  1060.4 9.8 custom-call.132
  1071.0 11.7 custom-call.133
  1083.1 10.0 custom-call.134
  1094.1 11.7 custom-call.135
  1105.9 9.8 custom-call.136
  1116.5 11.9 custom-call.137
  1133.9 11.3 while.3
  1145.2 40.1 %custom-call.138 = f32[1,4,128,128]{2,3,1,0:T(8,128)S(1)} custom-call(f32[1,4,128,128]{3,2,1,0:T(8,128)} %bitcast.372), custom_call_target="InvertDiagBlocksLowerTriangular" | custom-call | tf_op jit(solution)/shard_map/vmap(jit(_solve_triangular))/triangular_solve | solution.py:23
  1193.1 11.1 all-to-all-start
  1204.3 79.6 %reduce-scatter.2.cloned.1.call-done = f32[1,96,512]{2,1,0:T(8,128)} async-done(((f32[1,1536,512]{2,1,0:T(8,128)}), f32[1,96,512]{2,1,0:T(8,128)}) %reduce-scatter.2.cloned.1.call-update) | async-done | bytes 196624 | tf_op jit(solution)/shard_map/reduce_scatter | solution.py:62
  1285.5 80.8 %all-gather.5.cloned.1.call-done = bf16[1,1536,512]{2,1,0:T(8,128)(2,1)} async-done(((bf16[1,96,512]{2,1,0:T(8,128)(2,1)}), bf16[1,1536,512]{2,1,0:T(8,128)(2,1)}) %all-gather.5.cloned.1.call-update) | async-done | bytes 1572880 | tf_op jit(solution)/shard_map/all_gather | solution.py:65
  1369.9 218.2 %all-reduce.10.cloned.1.call-done = bf16[2,1,1536,512]{3,2,1,0:T(8,128)(2,1)} async-done(((bf16[2,1,1536,512]{3,2,1,0:T(8,128)(2,1)}), bf16[2,1,1536,512]{3,2,1,0:T(8,128)(2,1)}) %all-reduce.10.cloned.1.call-update) | async-done | bytes 3145744 | tf_op jit(solution)/shard_map/psum | solution.py:13
  (164 shorter events, 111.7 us)
Async XLA Ops:
  8.0 683.1 %all-reduce.6.cloned.1.call-start = ((), (), s32[]{:S(2)}) async-start(), calls=%async_computation.2 | async-start | bytes 18874368 | tf_op jit(solution)/shard_map/psum | solution.py:13
  48.6 0.7 copy-start.2
  48.6 0.7 copy-start.3
  48.7 824.0 %all-gather.3.cloned.1.call-start = ((), (), s32[]{:S(2)}) async-start(), calls=%async_computation.3 | async-start | bytes 1671168 | tf_op jit(solution)/shard_map/all_gather | solution.py:42
  49.2 985.7 %all-reduce.8.cloned.1.call-start = ((), (), s32[]{:S(2)}) async-start(), calls=%async_computation.4 | async-start | bytes 2097152 | tf_op jit(solution)/shard_map/psum | solution.py:52
  872.6 5.3 copy-start
  877.2 406.7 %reduce-scatter.2.cloned.1.call-start = ((), (), s32[]{:S(2)}) async-start(), calls=%async_computation.5 | async-start | bytes 3342336 | tf_op jit(solution)/shard_map/reduce_scatter | solution.py:62
  1193.1 92.4 %all-to-all-start = ((bf16[16,1,96,512]{3,2,1,0:T(8,128)(2,1)}), bf16[16,1,96,512]{3,2,1,0:T(8,128)(2,1)S(1)}, u32[]{:S(2)}, u32[]{:S(2)}) async-start(bf16[16,1,96,512]{3,2,1,0:T(8,128)(2,1)} %stack.8), calls=%async_computation | async-start | bytes 3145728 | tf_op jit(solution)/shard_map/all_to_all | solution.py:67
  1204.2 162.1 %all-gather.5.cloned.1.call-start = ((), (), s32[]{:S(2)}) async-start(), calls=%async_computation.6 | async-start | bytes 1671168 | tf_op jit(solution)/shard_map/all_gather | solution.py:65
  1285.4 302.7 %all-reduce.10.cloned.1.call-start = ((), (), s32[]{:S(2)}) async-start(), calls=%async_computation.7 | async-start | bytes 6291456 | tf_op jit(solution)/shard_map/psum | solution.py:13
  1366.3 221.8 %copy-start.1 = (bf16[1,1536,512]{2,1,0:T(8,128)(2,1)S(1)}, bf16[1,1536,512]{2,1,0:T(8,128)(2,1)}, u32[]{:S(2)}) copy-start(bf16[1,1536,512]{2,1,0:T(8,128)(2,1)} %all-gather.5.cloned.1.call-done) | copy-start | bytes 4718596
Sparse Core Ops, SparseCore 0:
  48.8 642.2 all-reduce.5
  1370.0 218.0 all-reduce.9
Sparse Core Ops, SparseCore 1:
  50.9 440.7 all-gather.2
  877.2 157.6 all-reduce.7
  1191.3 92.5 reduce-scatter.1
  1285.7 80.6 all-gather.4
